TPU v7x, 512 devices: a whole 4x8x8 slice. The times are simulated.
512 devices in a mesh: edp: 16 (over z, core), ep: 32 (over y, x).
Axes of the slice: x: 4, y: 8, z: 8, core: 2. Of those that a mesh axis runs over, the one named last changes fastest.
Arguments:
- token_acts: bfloat16 [16, 32, 2, 64, 1024], P('edp', 'ep'), may hold values from -6 to 6
- out_grad: bfloat16 [16, 32, 3584, 128], P('edp', 'ep'), may hold values from -0.59765625 to 0.59765625
- counts: int32 [16, 32, 2], P('edp', 'ep'), may hold values from 1 to 64, as said below
- params: float32 [32, 3584, 1024], P('ep', 'edp'), may hold values from -3 to 3
- first_moment: bfloat16 [32, 3584, 1024], P('ep', 'edp'), may hold values from -3 to 3
- second_moment: bfloat16 [32, 3584, 1024], P('ep', 'edp'), may hold values from 0.049804688 to 2
- old_expert: int32 [32], replicated, may hold values from 0 to 31, each once
- replica_of: int32 [32], replicated, may hold values from 0 to 31
- new_expert: int32 [32], replicated, may hold values from 0 to 31, each once
Outputs:
- update_step: float32 [32, 3584, 1024], P('ep', 'edp')
- new_first: bfloat16 [32, 3584, 1024], P('ep', 'edp')
- new_second: bfloat16 [32, 3584, 1024], P('ep', 'edp')
Inputs may be any that keep to these rules, and one draw needn't show every extreme that they name: `counts`: every slot has at least one live token; some slot is full and some slot has exactly one live token in every draw. `old_expert`: each expert appears exactly once. `new_expert`: each expert appears exactly once. `replica_of`: any expert may be served by any number of replica slots, its owner's included.
All inputs are finite; a program needn't handle non-finite values.
Results may differ from a plain program's by a relative error of at most 0.015.
Values may be sent and summed in bfloat16 or wider, within the bound.
A program may use at most 64 MiB of HBM per device.

v0:
```python
import jax
import jax.numpy as jnp
from jax import lax
from jax.sharding import PartitionSpec as P

beta_one = 0.9
beta_two = 0.95
bias_one = 0.9999734386011124
bias_two = 0.994079470779666
decay_rate = 0.1
adam_eps = 1e-08


def adam_update(weights, first_old, second_old, gradient):
    first_new = beta_one * first_old.astype(jnp.float32) + (1.0 - beta_one) * gradient
    second_new = beta_two * second_old.astype(jnp.float32) + (1.0 - beta_two) * gradient * gradient
    scaled = first_new / bias_one / (jnp.sqrt(second_new / bias_two) + adam_eps)
    step_new = -(scaled + decay_rate * weights)
    return (step_new, first_new.astype(jnp.bfloat16), second_new.astype(jnp.bfloat16))


def local(
    token_acts,
    out_grad,
    counts,
    params,
    first_moment,
    second_moment,
    old_expert,
    replica_of,
    new_expert,
):
    groups = lax.axis_size("edp")
    owners = lax.axis_size("ep")
    model_width = out_grad.shape[2]
    slot_count = token_acts.shape[2]
    tok_slot = token_acts.shape[3]
    hidden_units = token_acts.shape[4]
    row_count = model_width // groups
    piece_len = row_count * hidden_units // owners
    local_grad = out_grad[0, 0]
    local_counts = counts[0, 0]
    column = jnp.arange(slot_count * tok_slot, dtype=jnp.int32)
    slot_index = column // tok_slot
    live_limit = jnp.where(slot_index == 0, local_counts[0], local_counts[1])
    live_mask = column % tok_slot < live_limit
    masked = jnp.where(live_mask[None, :], local_grad, jnp.zeros_like(local_grad))
    received = lax.all_to_all(
        masked.reshape(groups, row_count, slot_count * tok_slot),
        "edp",
        split_axis=0,
        concat_axis=0,
        tiled=True,
    )
    arrived = lax.all_gather(token_acts[0], "edp", axis=0, tiled=True)
    count_here = arrived.shape[0]
    grad_block = received
    grad_block = grad_block.reshape(count_here, row_count, slot_count, tok_slot)
    slot_grads = jnp.einsum(
        "adst,astf->sdf", grad_block, arrived, preferred_element_type=jnp.float32
    )
    own_grad = slot_grads[0].reshape(owners, piece_len)
    replica_grad = slot_grads[1].reshape(owners, piece_len)
    sum_matrix = (replica_of[None, :] == old_expert[:, None]).astype(jnp.float32)
    move_matrix = (old_expert[None, :] == new_expert[:, None]).astype(jnp.float32)
    weights = params[0].reshape(owners, piece_len)
    first_old = first_moment[0].reshape(owners, piece_len)
    second_old = second_moment[0].reshape(owners, piece_len)
    replica_sent = lax.all_to_all(
        replica_grad.astype(jnp.bfloat16), "ep", split_axis=0, concat_axis=0, tiled=True
    ).astype(replica_grad.dtype)
    set_sums = jnp.dot(sum_matrix, replica_sent, precision=lax.Precision.HIGHEST)
    returned = lax.all_to_all(
        set_sums.astype(jnp.bfloat16), "ep", split_axis=0, concat_axis=0, tiled=True
    ).astype(set_sums.dtype)
    weights, first_old, second_old = adam_update(
        weights, first_old, second_old, own_grad + returned
    )
    weight_pieces = lax.all_to_all(weights, "ep", split_axis=0, concat_axis=0, tiled=True)
    first_pieces, second_pieces = (
        lax.all_to_all(first_old, "ep", split_axis=0, concat_axis=0, tiled=True),
        lax.all_to_all(second_old, "ep", split_axis=0, concat_axis=0, tiled=True),
    )
    placed_steps = jnp.dot(move_matrix, weight_pieces, precision=lax.Precision.HIGHEST)
    move_half = move_matrix.astype(jnp.bfloat16)
    placed_first = jnp.dot(move_half, first_pieces, preferred_element_type=jnp.float32).astype(
        jnp.bfloat16
    )
    placed_second = jnp.dot(move_half, second_pieces, preferred_element_type=jnp.float32).astype(
        jnp.bfloat16
    )
    final_steps = lax.all_to_all(placed_steps, "ep", split_axis=0, concat_axis=0, tiled=True)
    final_first, final_second = (
        lax.all_to_all(placed_first, "ep", split_axis=0, concat_axis=0, tiled=True),
        lax.all_to_all(placed_second, "ep", split_axis=0, concat_axis=0, tiled=True),
    )
    return (
        final_steps.reshape(1, row_count, hidden_units),
        final_first.reshape(1, row_count, hidden_units),
        final_second.reshape(1, row_count, hidden_units),
    )


def solution(mesh):
    return jax.shard_map(
        local,
        mesh=mesh,
        in_specs=(
            P("edp", "ep", None, None, None),
            P("edp", "ep", None, None),
            P("edp", "ep", None),
            P("ep", "edp", None),
            P("ep", "edp", None),
            P("ep", "edp", None),
            P(),
            P(),
            P(),
        ),
        out_specs=(P("ep", "edp", None), P("ep", "edp", None), P("ep", "edp", None)),
        check_vma=False,
    )
```

profile of v0, /device:TPU:2, one launch (start us, length us, event | category | flops | bytes accessed | tf_op | source)
XLA Modules:
  0.0 280.3 jit_solution(12393630941862970195)
XLA Ops:
  11.8 41.0 %all_to_all.77 = bf16[16,224,128]{2,1,0:T(8,128)(2,1)S(1)} all-to-all(bf16[16,224,128]{2,1,0:T(8,128)(2,1)S(1)} %broadcast_select_fusion), channel_id=1, replica_groups=mesh['edp'=16,'ep'=32] {'edp'}, dimensions={0} | all-to-all | bytes 1835008 | tf_op jit(solution)/shard_map/all_to_all | solution.py:48
  53.3 18.0 %all-gather.3.cloned.1.call-done = bf16[16,1,2,64,1024]{4,3,2,1,0:T(8,128)(2,1)} async-done(((bf16[1,1,2,64,1024]{4,3,2,1,0:T(8,128)(2,1)}), bf16[16,1,2,64,1024]{4,3,2,1,0:T(8,128)(2,1)}) %all-gather.3.cloned.1.call-update) | async-done | bytes 4194320 | tf_op jit(solution)/shard_map/all_gather | solution.py:55
  71.3 3.3 %fusion.5 = f32[2,224,1024]{2,1,0:T(8,128)S(1)} fusion(bf16[16,224,2,64]{1,3,2,0:T(8,128)(2,1)S(1)} %bitcast.32, bf16[16,1,2,64,1024]{4,3,2,1,0:T(8,128)(2,1)} %all-gather.3.cloned.1.call-done), kind=kOutput, calls=%fused_computation.9 | convolution fusion | flops 939524096 | bytes 6946816 | tf_op jit(solution)/shard_map/adst,astf->sdf/dot_general | solution.py:59
  75.7 3.3 %reduce.3 = bf16[32,7168]{1,0:T(8,128)(2,1)S(1)} reduce(bf16[32,1,7168]{2,1,0:T(2,128)(2,1)S(1)} %convert_element_type.77, bf16[]{:T(256)} %broadcast.125), dimensions={1}, to_apply=%convert_element_type.77.reduce_sub_computation | reduce | bytes 917506 | tf_op jit(solution)/shard_map/convert_element_type | solution.py:70
  79.3 25.9 %all_to_all.78 = bf16[32,2,3584]{2,1,0:T(2,128)(2,1)S(1)} all-to-all(bf16[32,2,3584]{2,1,0:T(2,128)(2,1)S(1)} %reshape.144), channel_id=1, replica_groups=mesh['edp'=16,'ep'=32] {'ep'}, dimensions={0} | all-to-all | bytes 917504 | tf_op jit(solution)/shard_map/all_to_all | solution.py:69
  107.8 5.6 %all-to-all-start.2 = ((bf16[32,2,3584]{2,1,0:T(2,128)(2,1)}), bf16[32,2,3584]{2,1,0:T(2,128)(2,1)S(1)}, u32[]{:S(2)}, u32[]{:S(2)}) async-start(bf16[32,2,3584]{2,1,0:T(2,128)(2,1)} %reshape.146), calls=%async_computation.2 | async-start | bytes 917504 | tf_op jit(solution)/shard_map/all_to_all | solution.py:73
  113.4 2.2 broadcast_multiply_fusion
  115.7 1.6 mul.76
  117.2 2.1 convert_multiply_fusion.1
  119.3 2.6 mul.67
  121.9 2.0 convert_multiply_fusion
  123.9 2.5 mul.71
  127.4 1.6 reshape_squeeze.2
  130.2 3.1 %fusion.32 = (bf16[32,1,7168]{2,0,1:T(8,128)(2,1)}, f32[32,1,7168]{2,0,1:T(8,128)S(1)}, bf16[32,1,7168]{2,0,1:T(8,128)(2,1)S(1)}) fusion(f32[32,1,7168]{2,0,1:T(8,128)} %mul.71, f32[32,1,7168]{2,0,1:T(8,128)S(1)} %reshape_squeeze.2, bf16[32,1,7168]{2,1,0:T(2,128)(2,1)} %reshape.147, f32[32,1,7168]{2,0,1:T(8,128)S(1)} %mul.76, f32[32,1,7168]{2,0,1:T(8,128)} %mul.67), kind=kLoop, calls=%fused_computation.47 | loop fusion | flops 3440640 | bytes 5963776 | tf_op jit(solution)/shard_map/convert_element_type | solution.py:19
  133.3 1.9 reduce.7
  136.3 9.8 %all-to-all-start.7 = ((bf16[32,2,3584]{2,1,0:T(2,128)(2,1)}), bf16[32,2,3584]{2,1,0:T(2,128)(2,1)S(1)}, u32[]{:S(2)}, u32[]{:S(2)}) async-start(bf16[32,2,3584]{2,1,0:T(2,128)(2,1)} %reshape.152), calls=%async_computation.7 | async-start | bytes 917504 | tf_op jit(solution)/shard_map/all_to_all | solution.py:82
  148.0 12.1 %all-to-all-done.7 = bf16[32,2,3584]{2,1,0:T(2,128)(2,1)S(1)} async-done(((bf16[32,2,3584]{2,1,0:T(2,128)(2,1)}), bf16[32,2,3584]{2,1,0:T(2,128)(2,1)S(1)}, u32[]{:S(2)}, u32[]{:S(2)}) %all-to-all-start.7) | async-done | bytes 458784 | tf_op jit(solution)/shard_map/all_to_all | solution.py:82
  160.1 5.7 %all-to-all-start.5 = ((bf16[32,2,3584]{2,1,0:T(2,128)(2,1)}), bf16[32,2,3584]{2,1,0:T(2,128)(2,1)S(1)}, u32[]{:S(2)}, u32[]{:S(2)}) async-start(bf16[32,2,3584]{2,1,0:T(2,128)(2,1)} %reshape.148), calls=%async_computation.5 | async-start | bytes 917504 | tf_op jit(solution)/shard_map/all_to_all | solution.py:81
  168.6 10.7 %all-to-all-done.5 = bf16[32,2,3584]{2,1,0:T(2,128)(2,1)S(1)} async-done(((bf16[32,2,3584]{2,1,0:T(2,128)(2,1)}), bf16[32,2,3584]{2,1,0:T(2,128)(2,1)S(1)}, u32[]{:S(2)}, u32[]{:S(2)}) %all-to-all-start.5) | async-done | bytes 458784 | tf_op jit(solution)/shard_map/all_to_all | solution.py:81
  179.3 5.6 %all-to-all-start.8 = ((bf16[32,2,3584]{2,1,0:T(2,128)(2,1)}), bf16[32,2,3584]{2,1,0:T(2,128)(2,1)S(1)}, u32[]{:S(2)}, u32[]{:S(2)}) async-start(bf16[32,2,3584]{2,1,0:T(2,128)(2,1)} %reshape.154), calls=%async_computation.8 | async-start | bytes 917504 | tf_op jit(solution)/shard_map/all_to_all | solution.py:95
  184.9 1.9 copy.35
  186.7 11.1 %all-to-all-done.8 = bf16[32,2,3584]{2,1,0:T(2,128)(2,1)S(1)} async-done(((bf16[32,2,3584]{2,1,0:T(2,128)(2,1)}), bf16[32,2,3584]{2,1,0:T(2,128)(2,1)S(1)}, u32[]{:S(2)}, u32[]{:S(2)}) %all-to-all-start.8) | async-done | bytes 458784 | tf_op jit(solution)/shard_map/all_to_all | solution.py:95
  197.9 5.6 %all-to-all-start.3 = ((f32[32,1,7168]{2,1,0:T(1,128)}), f32[32,1,7168]{2,1,0:T(1,128)S(1)}, u32[]{:S(2)}, u32[]{:S(2)}) async-start(f32[32,1,7168]{2,1,0:T(1,128)} %copy.35), calls=%async_computation.3 | async-start | bytes 1835008 | tf_op jit(solution)/shard_map/all_to_all | solution.py:79
  206.1 19.8 %all-to-all-done.3 = f32[32,1,7168]{2,1,0:T(1,128)S(1)} async-done(((f32[32,1,7168]{2,1,0:T(1,128)}), f32[32,1,7168]{2,1,0:T(1,128)S(1)}, u32[]{:S(2)}, u32[]{:S(2)}) %all-to-all-start.3) | async-done | bytes 917536 | tf_op jit(solution)/shard_map/all_to_all | solution.py:79
  225.9 5.6 %all-to-all-start.6 = ((bf16[32,2,3584]{2,1,0:T(2,128)(2,1)}), bf16[32,2,3584]{2,1,0:T(2,128)(2,1)S(1)}, u32[]{:S(2)}, u32[]{:S(2)}) async-start(bf16[32,2,3584]{2,1,0:T(2,128)(2,1)} %reshape.150), calls=%async_computation.6 | async-start | bytes 917504 | tf_op jit(solution)/shard_map/all_to_all | solution.py:94
  232.1 1.9 copy.36
  234.0 9.8 %all-to-all-done.6 = bf16[32,2,3584]{2,1,0:T(2,128)(2,1)S(1)} async-done(((bf16[32,2,3584]{2,1,0:T(2,128)(2,1)}), bf16[32,2,3584]{2,1,0:T(2,128)(2,1)S(1)}, u32[]{:S(2)}, u32[]{:S(2)}) %all-to-all-start.6) | async-done | bytes 458784 | tf_op jit(solution)/shard_map/all_to_all | solution.py:94
  243.7 5.6 %all-to-all-start.4 = ((f32[32,1,7168]{2,1,0:T(1,128)}), f32[32,1,7168]{2,1,0:T(1,128)S(1)}, u32[]{:S(2)}, u32[]{:S(2)}) async-start(f32[32,1,7168]{2,1,0:T(1,128)} %copy.36), calls=%async_computation.4 | async-start | bytes 1835008 | tf_op jit(solution)/shard_map/all_to_all | solution.py:92
  249.7 2.7 reduce.2
  254.1 2.7 reduce.1
  258.1 12.1 %all-to-all-done.4 = f32[32,1,7168]{2,1,0:T(1,128)S(1)} async-done(((f32[32,1,7168]{2,1,0:T(1,128)}), f32[32,1,7168]{2,1,0:T(1,128)S(1)}, u32[]{:S(2)}, u32[]{:S(2)}) %all-to-all-start.4) | async-done | bytes 917536 | tf_op jit(solution)/shard_map/all_to_all | solution.py:92
  270.2 2.2 reduce
  (40 shorter events, 24.5 us)
Async XLA Ops:
  7.2 64.1 %all-gather.3.cloned.1.call-start = ((), (), s32[]{:S(2)}) async-start(), calls=%async_computation.9 | async-start | bytes 4456448 | tf_op jit(solution)/shard_map/all_gather | solution.py:55
  74.7 30.9 %copy-start = (s32[32]{0:T(128)S(1)}, s32[32]{0:T(128)}, u32[]{:S(2)}) copy-start(s32[32]{0:T(128)} %param.15) | copy-start | bytes 388
  74.7 30.9 %copy-start.2 = (s32[32]{0:T(128)S(1)}, s32[32]{0:T(128)}, u32[]{:S(2)}) copy-start(s32[32]{0:T(128)} %param.16) | copy-start | bytes 388
  107.8 21.2 %all-to-all-start.2 = ((bf16[32,2,3584]{2,1,0:T(2,128)(2,1)}), bf16[32,2,3584]{2,1,0:T(2,128)(2,1)S(1)}, u32[]{:S(2)}, u32[]{:S(2)}) async-start(bf16[32,2,3584]{2,1,0:T(2,128)(2,1)} %reshape.146), calls=%async_computation.2 | async-start | bytes 917504 | tf_op jit(solution)/shard_map/all_to_all | solution.py:73
  133.3 33.0 %copy-start.1 = (s32[32]{0:T(128)S(1)}, s32[32]{0:T(128)}, u32[]{:S(2)}) copy-start(s32[32]{0:T(128)} %param.17) | copy-start | bytes 388
  136.3 23.9 %all-to-all-start.7 = ((bf16[32,2,3584]{2,1,0:T(2,128)(2,1)}), bf16[32,2,3584]{2,1,0:T(2,128)(2,1)S(1)}, u32[]{:S(2)}, u32[]{:S(2)}) async-start(bf16[32,2,3584]{2,1,0:T(2,128)(2,1)} %reshape.152), calls=%async_computation.7 | async-start | bytes 917504 | tf_op jit(solution)/shard_map/all_to_all | solution.py:82
  160.1 19.2 %all-to-all-start.5 = ((bf16[32,2,3584]{2,1,0:T(2,128)(2,1)}), bf16[32,2,3584]{2,1,0:T(2,128)(2,1)S(1)}, u32[]{:S(2)}, u32[]{:S(2)}) async-start(bf16[32,2,3584]{2,1,0:T(2,128)(2,1)} %reshape.148), calls=%async_computation.5 | async-start | bytes 917504 | tf_op jit(solution)/shard_map/all_to_all | solution.py:81
  179.3 18.6 %all-to-all-start.8 = ((bf16[32,2,3584]{2,1,0:T(2,128)(2,1)}), bf16[32,2,3584]{2,1,0:T(2,128)(2,1)S(1)}, u32[]{:S(2)}, u32[]{:S(2)}) async-start(bf16[32,2,3584]{2,1,0:T(2,128)(2,1)} %reshape.154), calls=%async_computation.8 | async-start | bytes 917504 | tf_op jit(solution)/shard_map/all_to_all | solution.py:95
  197.9 28.0 %all-to-all-start.3 = ((f32[32,1,7168]{2,1,0:T(1,128)}), f32[32,1,7168]{2,1,0:T(1,128)S(1)}, u32[]{:S(2)}, u32[]{:S(2)}) async-start(f32[32,1,7168]{2,1,0:T(1,128)} %copy.35), calls=%async_computation.3 | async-start | bytes 1835008 | tf_op jit(solution)/shard_map/all_to_all | solution.py:79
  225.9 17.8 %all-to-all-start.6 = ((bf16[32,2,3584]{2,1,0:T(2,128)(2,1)}), bf16[32,2,3584]{2,1,0:T(2,128)(2,1)S(1)}, u32[]{:S(2)}, u32[]{:S(2)}) async-start(bf16[32,2,3584]{2,1,0:T(2,128)(2,1)} %reshape.150), calls=%async_computation.6 | async-start | bytes 917504 | tf_op jit(solution)/shard_map/all_to_all | solution.py:94
  243.7 26.5 %all-to-all-start.4 = ((f32[32,1,7168]{2,1,0:T(1,128)}), f32[32,1,7168]{2,1,0:T(1,128)S(1)}, u32[]{:S(2)}, u32[]{:S(2)}) async-start(f32[32,1,7168]{2,1,0:T(1,128)} %copy.36), calls=%async_computation.4 | async-start | bytes 1835008 | tf_op jit(solution)/shard_map/all_to_all | solution.py:92
Sparse Core Ops, SparseCore 0:
  10.1 61.1 all-gather.2
where the time goes:
time: 282 us; the launch traced here: 280 us
  waiting for transfers between devices  94.3 us (33%)
  blocking collectives  66.9 us (24%)
  starting transfers between devices  43.4 us (15%)
  local copies, waits for them, and re-layouts  28.2 us (10%)
  other arithmetic  28.2 us (10%)
  between operations  14.3 us (5%)
  matrix products  4.97 us (2%)
    all_to_all x1, blocking collectives, local(): lax.all_to_all(masked.reshape(groups, row_count, slot_count * tok_slot),...  41 us
    all_to_all x1, blocking collectives, local(): lax.all_to_all(replica_grad.astype(jnp.bfloat16), 'ep', split_axis=0, con...  25.9 us
    all_to_all x1, waiting for transfers between devices, local(): lax.all_to_all(weights, 'ep', split_axis=0, concat_axis=0, tiled=True)  19.8 us
    all_gather x1, waiting for transfers between devices, local(): arrived = lax.all_gather(token_acts[0], 'edp', axis=0, tiled=True)  18 us
    all_to_all x1, waiting for transfers between devices, local(): lax.all_to_all(second_old, 'ep', split_axis=0, concat_axis=0, tiled=True)  12.1 us
    all_to_all x1, waiting for transfers between devices, local(): lax.all_to_all(placed_steps, 'ep', split_axis=0, concat_axis=0, tiled=True)  12.1 us
    all_to_all x1, waiting for transfers between devices, local(): lax.all_to_all(placed_second, 'ep', split_axis=0, concat_axis=0, tiled=True)  11.1 us
    all_to_all x1, waiting for transfers between devices, local(): lax.all_to_all(first_old, 'ep', split_axis=0, concat_axis=0, tiled=True)  10.7 us
  transfers between devices with their start and end apart: 8, of which 7 were waited for; matrix products, arithmetic and copies ran while one was open for 14% of the time, Pallas kernels for 0%

commit v1 on v0

--- a/solution.py
+++ b/solution.py
@@ -52,7 +52,9 @@
         concat_axis=0,
         tiled=True,
     )
-    arrived = lax.all_gather(token_acts[0], "edp", axis=0, tiled=True)
+    arrived = jnp.concatenate(
+        lax.all_to_all(jnp.stack([token_acts[0]] * lax.axis_size("edp")), "edp", 0, 0), axis=0
+    )
     count_here = arrived.shape[0]
     grad_block = received
     grad_block = grad_block.reshape(count_here, row_count, slot_count, tok_slot)

time: 282 us -> 345 us (1.22)
  waiting for transfers between devices: 94.3 us -> 169 us
  between operations: 14.3 us -> 0.93 us
  blocking collectives: 66.9 us -> 60.4 us
  starting transfers between devices: 43.4 us -> 47.7 us
  local copies, waits for them, and re-layouts: 28.2 us -> 31.7 us
    all_to_all x0 -> x1, waiting for transfers between devices: none -> 93.7 us  [local(): lax.all_to_all(jnp.stack([token_acts[0]] * lax.axis_size('edp')), 'edp',...]
    all_gather x1 -> x0, waiting for transfers between devices: 18 us -> none  [local(): arrived = lax.all_gather(token_acts[0], 'edp', axis=0, tiled=True)]
    all_to_all x1, blocking collectives: 41 us -> 35.1 us  [local(): lax.all_to_all(masked.reshape(groups, row_count, slot_count * tok_slot),...]
    all_to_all x0 -> x1, starting transfers between devices: none -> 4.53 us  [local(): lax.all_to_all(jnp.stack([token_acts[0]] * lax.axis_size('edp')), 'edp',...]
    all_to_all x1, starting transfers between devices: 9.78 us -> 5.57 us  [local(): lax.all_to_all(second_old, 'ep', split_axis=0, concat_axis=0, tiled=True)]
    all_to_all x1, starting transfers between devices: 5.74 us -> 9.78 us  [local(): lax.all_to_all(first_old, 'ep', split_axis=0, concat_axis=0, tiled=True)]
    another operation x0 -> x1, local copies, waits for them, and re-layouts: none -> 3.45 us  [local(): jnp.stack([token_acts[0]] * lax.axis_size('edp'))]
  transfers between devices with their start and end apart: 8 -> 8, of which waited for: 7 -> 7; matrix products, arithmetic and copies ran while one was open for 14% -> 11% of each run, Pallas kernels for 0% -> 0%
where the time goes in v1:
time: 345 us; the launch traced here: 343 us
  waiting for transfers between devices  169 us (49%)
  blocking collectives  60.4 us (18%)
  starting transfers between devices  47.7 us (14%)
  local copies, waits for them, and re-layouts  31.7 us (9%)
  other arithmetic  28.2 us (8%)
  matrix products  4.96 us (1%)
    all_to_all x1, waiting for transfers between devices, local(): lax.all_to_all(jnp.stack([token_acts[0]] * lax.axis_size('edp')), 'edp',...  93.7 us
    all_to_all x1, blocking collectives, local(): lax.all_to_all(masked.reshape(groups, row_count, slot_count * tok_slot),...  35.1 us
    all_to_all x1, blocking collectives, local(): lax.all_to_all(replica_grad.astype(jnp.bfloat16), 'ep', split_axis=0, con...  25.3 us
    all_to_all x1, waiting for transfers between devices, local(): lax.all_to_all(weights, 'ep', split_axis=0, concat_axis=0, tiled=True)  19.8 us
    all_to_all x1, waiting for transfers between devices, local(): lax.all_to_all(placed_steps, 'ep', split_axis=0, concat_axis=0, tiled=True)  12.1 us
    all_to_all x1, waiting for transfers between devices, local(): lax.all_to_all(first_old, 'ep', split_axis=0, concat_axis=0, tiled=True)  12.1 us
    all_to_all x1, waiting for transfers between devices, local(): lax.all_to_all(placed_first, 'ep', split_axis=0, concat_axis=0, tiled=True)  11.1 us
    all_to_all x1, waiting for transfers between devices, local(): lax.all_to_all(second_old, 'ep', split_axis=0, concat_axis=0, tiled=True)  10.7 us
  transfers between devices with their start and end apart: 8, of which 7 were waited for; matrix products, arithmetic and copies ran while one was open for 11% of the time, Pallas kernels for 0%

profile of v1, /device:TPU:2, one launch (start us, length us, event | category | flops | bytes accessed | tf_op | source)
XLA Modules:
  0.0 343.2 jit_solution(15834259271180663849)
XLA Ops:
  4.5 35.1 %all_to_all.82 = bf16[16,224,128]{2,1,0:T(8,128)(2,1)S(1)} all-to-all(bf16[16,224,128]{2,1,0:T(8,128)(2,1)S(1)} %broadcast_select_fusion), channel_id=1, replica_groups=mesh['edp'=16,'ep'=32] {'edp'}, dimensions={0} | all-to-all | bytes 1835008 | tf_op jit(solution)/shard_map/all_to_all | solution.py:48
  39.6 3.5 %stack.3 = bf16[16,1,2,64,1024]{4,3,2,1,0:T(8,128)(2,1)} broadcast(bf16[2,64,1024]{2,1,0:T(8,128)(2,1)} %bitcast.35), dimensions={2,3,4} | broadcast | bytes 4456448 | tf_op jit(solution)/shard_map/stack | solution.py:56
  43.1 4.5 %all-to-all-start.1 = ((bf16[16,1,2,64,1024]{4,3,2,1,0:T(8,128)(2,1)}), bf16[16,1,2,64,1024]{4,3,2,1,0:T(8,128)(2,1)}, u32[]{:S(2)}, u32[]{:S(2)}) async-start(bf16[16,1,2,64,1024]{4,3,2,1,0:T(8,128)(2,1)} %stack.3), calls=%async_computation.1 | async-start | bytes 8388608 | tf_op jit(solution)/shard_map/all_to_all | solution.py:56
  48.1 93.7 %all-to-all-done.1 = bf16[16,1,2,64,1024]{4,3,2,1,0:T(8,128)(2,1)} async-done(((bf16[16,1,2,64,1024]{4,3,2,1,0:T(8,128)(2,1)}), bf16[16,1,2,64,1024]{4,3,2,1,0:T(8,128)(2,1)}, u32[]{:S(2)}, u32[]{:S(2)}) %all-to-all-start.1) | async-done | bytes 4194336 | tf_op jit(solution)/shard_map/all_to_all | solution.py:56
  141.9 3.3 fusion.5
  146.3 3.3 reduce.3
  149.9 25.3 %all_to_all.83 = bf16[32,2,3584]{2,1,0:T(2,128)(2,1)S(1)} all-to-all(bf16[32,2,3584]{2,1,0:T(2,128)(2,1)S(1)} %reshape.150), channel_id=1, replica_groups=mesh['edp'=16,'ep'=32] {'ep'}, dimensions={0} | all-to-all | bytes 917504 | tf_op jit(solution)/shard_map/all_to_all | solution.py:71
  177.8 5.6 %all-to-all-start.3 = ((bf16[32,2,3584]{2,1,0:T(2,128)(2,1)}), bf16[32,2,3584]{2,1,0:T(2,128)(2,1)S(1)}, u32[]{:S(2)}, u32[]{:S(2)}) async-start(bf16[32,2,3584]{2,1,0:T(2,128)(2,1)} %reshape.152), calls=%async_computation.3 | async-start | bytes 917504 | tf_op jit(solution)/shard_map/all_to_all | solution.py:75
  183.4 2.1 convert_multiply_fusion.1
  187.1 2.1 convert_multiply_fusion
  189.1 2.5 mul.71
  191.6 2.2 broadcast_multiply_fusion
  193.9 2.6 mul.76
  200.2 3.1 fusion.32
  203.3 1.9 reduce.5
  206.3 9.8 %all-to-all-start.6 = ((bf16[32,2,3584]{2,1,0:T(2,128)(2,1)}), bf16[32,2,3584]{2,1,0:T(2,128)(2,1)S(1)}, u32[]{:S(2)}, u32[]{:S(2)}) async-start(bf16[32,2,3584]{2,1,0:T(2,128)(2,1)} %reshape.154), calls=%async_computation.6 | async-start | bytes 917504 | tf_op jit(solution)/shard_map/all_to_all | solution.py:83
  218.0 12.1 %all-to-all-done.6 = bf16[32,2,3584]{2,1,0:T(2,128)(2,1)S(1)} async-done(((bf16[32,2,3584]{2,1,0:T(2,128)(2,1)}), bf16[32,2,3584]{2,1,0:T(2,128)(2,1)S(1)}, u32[]{:S(2)}, u32[]{:S(2)}) %all-to-all-start.6) | async-done | bytes 458784 | tf_op jit(solution)/shard_map/all_to_all | solution.py:83
  230.1 5.6 %all-to-all-start.8 = ((bf16[32,2,3584]{2,1,0:T(2,128)(2,1)}), bf16[32,2,3584]{2,1,0:T(2,128)(2,1)S(1)}, u32[]{:S(2)}, u32[]{:S(2)}) async-start(bf16[32,2,3584]{2,1,0:T(2,128)(2,1)} %reshape.158), calls=%async_computation.8 | async-start | bytes 917504 | tf_op jit(solution)/shard_map/all_to_all | solution.py:84
  238.3 10.7 %all-to-all-done.8 = bf16[32,2,3584]{2,1,0:T(2,128)(2,1)S(1)} async-done(((bf16[32,2,3584]{2,1,0:T(2,128)(2,1)}), bf16[32,2,3584]{2,1,0:T(2,128)(2,1)S(1)}, u32[]{:S(2)}, u32[]{:S(2)}) %all-to-all-start.8) | async-done | bytes 458784 | tf_op jit(solution)/shard_map/all_to_all | solution.py:84
  249.1 5.6 %all-to-all-start.7 = ((bf16[32,2,3584]{2,1,0:T(2,128)(2,1)}), bf16[32,2,3584]{2,1,0:T(2,128)(2,1)S(1)}, u32[]{:S(2)}, u32[]{:S(2)}) async-start(bf16[32,2,3584]{2,1,0:T(2,128)(2,1)} %reshape.156), calls=%async_computation.7 | async-start | bytes 917504 | tf_op jit(solution)/shard_map/all_to_all | solution.py:96
  254.6 1.9 copy.32
  256.5 11.1 %all-to-all-done.7 = bf16[32,2,3584]{2,1,0:T(2,128)(2,1)S(1)} async-done(((bf16[32,2,3584]{2,1,0:T(2,128)(2,1)}), bf16[32,2,3584]{2,1,0:T(2,128)(2,1)S(1)}, u32[]{:S(2)}, u32[]{:S(2)}) %all-to-all-start.7) | async-done | bytes 458784 | tf_op jit(solution)/shard_map/all_to_all | solution.py:96
  267.6 5.6 %all-to-all-start.4 = ((f32[32,1,7168]{2,1,0:T(1,128)}), f32[32,1,7168]{2,1,0:T(1,128)S(1)}, u32[]{:S(2)}, u32[]{:S(2)}) async-start(f32[32,1,7168]{2,1,0:T(1,128)} %copy.32), calls=%async_computation.4 | async-start | bytes 1835008 | tf_op jit(solution)/shard_map/all_to_all | solution.py:81
  275.9 19.8 %all-to-all-done.4 = f32[32,1,7168]{2,1,0:T(1,128)S(1)} async-done(((f32[32,1,7168]{2,1,0:T(1,128)}), f32[32,1,7168]{2,1,0:T(1,128)S(1)}, u32[]{:S(2)}, u32[]{:S(2)}) %all-to-all-start.4) | async-done | bytes 917536 | tf_op jit(solution)/shard_map/all_to_all | solution.py:81
  295.6 5.6 %all-to-all-start.9 = ((bf16[32,2,3584]{2,1,0:T(2,128)(2,1)}), bf16[32,2,3584]{2,1,0:T(2,128)(2,1)S(1)}, u32[]{:S(2)}, u32[]{:S(2)}) async-start(bf16[32,2,3584]{2,1,0:T(2,128)(2,1)} %reshape.160), calls=%async_computation.9 | async-start | bytes 917504 | tf_op jit(solution)/shard_map/all_to_all | solution.py:97
  301.9 1.9 copy.33
  303.7 9.8 %all-to-all-done.9 = bf16[32,2,3584]{2,1,0:T(2,128)(2,1)S(1)} async-done(((bf16[32,2,3584]{2,1,0:T(2,128)(2,1)}), bf16[32,2,3584]{2,1,0:T(2,128)(2,1)S(1)}, u32[]{:S(2)}, u32[]{:S(2)}) %all-to-all-start.9) | async-done | bytes 458784 | tf_op jit(solution)/shard_map/all_to_all | solution.py:97
  313.5 5.6 %all-to-all-start.5 = ((f32[32,1,7168]{2,1,0:T(1,128)}), f32[32,1,7168]{2,1,0:T(1,128)S(1)}, u32[]{:S(2)}, u32[]{:S(2)}) async-start(f32[32,1,7168]{2,1,0:T(1,128)} %copy.33), calls=%async_computation.5 | async-start | bytes 1835008 | tf_op jit(solution)/shard_map/all_to_all | solution.py:94
  319.5 2.7 reduce.1
  323.8 2.7 reduce.2
  327.9 12.1 %all-to-all-done.5 = f32[32,1,7168]{2,1,0:T(1,128)S(1)} async-done(((f32[32,1,7168]{2,1,0:T(1,128)}), f32[32,1,7168]{2,1,0:T(1,128)S(1)}, u32[]{:S(2)}, u32[]{:S(2)}) %all-to-all-start.5) | async-done | bytes 917536 | tf_op jit(solution)/shard_map/all_to_all | solution.py:94
  340.0 2.2 reduce
  (40 shorter events, 27.0 us)
Async XLA Ops:
  43.1 98.8 %all-to-all-start.1 = ((bf16[16,1,2,64,1024]{4,3,2,1,0:T(8,128)(2,1)}), bf16[16,1,2,64,1024]{4,3,2,1,0:T(8,128)(2,1)}, u32[]{:S(2)}, u32[]{:S(2)}) async-start(bf16[16,1,2,64,1024]{4,3,2,1,0:T(8,128)(2,1)} %stack.3), calls=%async_computation.1 | async-start | bytes 8388608 | tf_op jit(solution)/shard_map/all_to_all | solution.py:56
  145.2 30.3 %copy-start = (s32[32]{0:T(128)S(1)}, s32[32]{0:T(128)}, u32[]{:S(2)}) copy-start(s32[32]{0:T(128)} %param.15) | copy-start | bytes 388
  145.3 30.3 %copy-start.2 = (s32[32]{0:T(128)S(1)}, s32[32]{0:T(128)}, u32[]{:S(2)}) copy-start(s32[32]{0:T(128)} %param.16) | copy-start | bytes 388
  177.8 21.2 %all-to-all-start.3 = ((bf16[32,2,3584]{2,1,0:T(2,128)(2,1)}), bf16[32,2,3584]{2,1,0:T(2,128)(2,1)S(1)}, u32[]{:S(2)}, u32[]{:S(2)}) async-start(bf16[32,2,3584]{2,1,0:T(2,128)(2,1)} %reshape.152), calls=%async_computation.3 | async-start | bytes 917504 | tf_op jit(solution)/shard_map/all_to_all | solution.py:75
  203.3 32.7 %copy-start.1 = (s32[32]{0:T(128)S(1)}, s32[32]{0:T(128)}, u32[]{:S(2)}) copy-start(s32[32]{0:T(128)} %param.17) | copy-start | bytes 388
  206.3 23.8 %all-to-all-start.6 = ((bf16[32,2,3584]{2,1,0:T(2,128)(2,1)}), bf16[32,2,3584]{2,1,0:T(2,128)(2,1)S(1)}, u32[]{:S(2)}, u32[]{:S(2)}) async-start(bf16[32,2,3584]{2,1,0:T(2,128)(2,1)} %reshape.154), calls=%async_computation.6 | async-start | bytes 917504 | tf_op jit(solution)/shard_map/all_to_all | solution.py:83
  230.1 19.0 %all-to-all-start.8 = ((bf16[32,2,3584]{2,1,0:T(2,128)(2,1)}), bf16[32,2,3584]{2,1,0:T(2,128)(2,1)S(1)}, u32[]{:S(2)}, u32[]{:S(2)}) async-start(bf16[32,2,3584]{2,1,0:T(2,128)(2,1)} %reshape.158), calls=%async_computation.8 | async-start | bytes 917504 | tf_op jit(solution)/shard_map/all_to_all | solution.py:84
  249.1 18.6 %all-to-all-start.7 = ((bf16[32,2,3584]{2,1,0:T(2,128)(2,1)}), bf16[32,2,3584]{2,1,0:T(2,128)(2,1)S(1)}, u32[]{:S(2)}, u32[]{:S(2)}) async-start(bf16[32,2,3584]{2,1,0:T(2,128)(2,1)} %reshape.156), calls=%async_computation.7 | async-start | bytes 917504 | tf_op jit(solution)/shard_map/all_to_all | solution.py:96
  267.6 28.0 %all-to-all-start.4 = ((f32[32,1,7168]{2,1,0:T(1,128)}), f32[32,1,7168]{2,1,0:T(1,128)S(1)}, u32[]{:S(2)}, u32[]{:S(2)}) async-start(f32[32,1,7168]{2,1,0:T(1,128)} %copy.32), calls=%async_computation.4 | async-start | bytes 1835008 | tf_op jit(solution)/shard_map/all_to_all | solution.py:81
  295.6 17.8 %all-to-all-start.9 = ((bf16[32,2,3584]{2,1,0:T(2,128)(2,1)}), bf16[32,2,3584]{2,1,0:T(2,128)(2,1)S(1)}, u32[]{:S(2)}, u32[]{:S(2)}) async-start(bf16[32,2,3584]{2,1,0:T(2,128)(2,1)} %reshape.160), calls=%async_computation.9 | async-start | bytes 917504 | tf_op jit(solution)/shard_map/all_to_all | solution.py:97
  313.5 26.5 %all-to-all-start.5 = ((f32[32,1,7168]{2,1,0:T(1,128)}), f32[32,1,7168]{2,1,0:T(1,128)S(1)}, u32[]{:S(2)}, u32[]{:S(2)}) async-start(f32[32,1,7168]{2,1,0:T(1,128)} %copy.33), calls=%async_computation.5 | async-start | bytes 1835008 | tf_op jit(solution)/shard_map/all_to_all | solution.py:94
